TPU v7x, 32 devices: a whole 2x2x4 slice. The times are simulated.
32 devices in a mesh: section: 2 (over y), batch: 4 (over x, core), tensor: 4 (over z).
Axes of the slice: x: 2, y: 2, z: 4, core: 2. Of those that a mesh axis runs over, the one named last changes fastest.
Arguments:
- ids_beam: int32 [8, 256], P('batch'), may hold values from 0 to 15999
- beam_map: int32 [8], replicated, may hold values from 0 to 7, each once
- lengths: int32 [8], replicated, may hold values from 1 to 256, 1536 in all
- embed_table: bfloat16 [16000, 4096], P(None, ('section', 'tensor')), may hold values from -6 to 6
- gain_attn: bfloat16 [2, 4096], P('section'), may hold values from 0.099609375 to 1.8984375
- w_query: bfloat16 [2, 4096, 4096], P('section', None, 'tensor'), may hold values from -1 to 1
- w_key: bfloat16 [2, 4096, 4096], P('section', None, 'tensor'), may hold values from -3 to 3
- w_value: bfloat16 [2, 4096, 4096], P('section', None, 'tensor'), may hold values from -0.09375 to 0.09375
- w_out: bfloat16 [2, 4096, 4096], P('section', 'tensor'), may hold values from -0.09375 to 0.09375
- gain_mlp: bfloat16 [2, 4096], P('section'), may hold values from 0.099609375 to 1.8984375
- w_gate: bfloat16 [2, 4096, 8192], P('section', None, 'tensor'), may hold values from -0.09375 to 0.09375
- w_up: bfloat16 [2, 4096, 8192], P('section', None, 'tensor'), may hold values from -0.09375 to 0.09375
- w_down: bfloat16 [2, 8192, 4096], P('section', 'tensor'), may hold values from -0.0625 to 0.0625
- final_gain: bfloat16 [4096], replicated, may hold values from 0.099609375 to 1.8984375
- score_weight: bfloat16 [4096], replicated, may hold values from -0.09375 to 0.09375
Outputs:
- residual_output: bfloat16 [8, 256, 4096], P('batch', 'tensor', 'section')
- scores: float32 [8], P('batch')
Inputs may be any that keep to these rules, and one draw needn't show every extreme that they name: A permutation: candidate c reads row beam_map[c] of ids_beam. `lengths`: the score is read at the last token before the padding.
All inputs are finite; a program needn't handle non-finite values.
Results may differ from a plain program's by a relative error of at most 0.04.
Values may be sent and summed in bfloat16 or wider, within the bound.
No kernel may reach another device: no remote copies, remote signals or barrier semaphores. Data moves between devices by JAX's collectives and lax.ppermute only.
A program may use at most 256 MiB of HBM per device.

v0:
```python
import jax
import jax.numpy as jnp
from jax import lax
from jax.sharding import PartitionSpec as P

HEAD_DIM = 128
EPSILON = 1e-05
ROTARY_FREQ_BASE = 10000.0


def shifted(value, axis, steps):
    count = lax.axis_size(axis)
    leading, last = (max(0, -steps), min(count, count - steps))
    return lax.ppermute(value, axis, [(source, source + steps) for source in range(leading, last)])


def rms_norm(hidden, scale_gain):
    values = hidden.astype(jnp.float32)
    inverse = lax.rsqrt(jnp.mean(values * values, axis=-1, keepdims=True) + EPSILON)
    return (values * inverse * scale_gain.astype(jnp.float32)).astype(jnp.bfloat16)


def rope_tables(length, head_dim):
    half_dim = head_dim // 2
    frequency = ROTARY_FREQ_BASE ** (-(jnp.arange(half_dim, dtype=jnp.float32) / half_dim))
    angles = jnp.arange(length, dtype=jnp.float32)[:, None] * frequency[None, :]
    return (jnp.cos(angles), jnp.sin(angles))


def rotate(values, cosine_table, sine_table):
    half_dim = values.shape[-1] // 2
    first_half = values[..., :half_dim]
    second_half = values[..., half_dim:]
    cosine_wide = cosine_table[:, None, :]
    sine_wide = sine_table[:, None, :]
    return jnp.concatenate(
        [
            first_half * cosine_wide - second_half * sine_wide,
            second_half * cosine_wide + first_half * sine_wide,
        ],
        axis=-1,
    )


def final_score(last_row, final_gain, score_weight):
    values = last_row.astype(jnp.float32)
    inverse = lax.rsqrt(jnp.mean(values * values, axis=-1, keepdims=True) + EPSILON)
    return jnp.sum(
        values * inverse * final_gain.astype(jnp.float32) * score_weight.astype(jnp.float32),
        axis=-1,
    )


def project_three(normed, w_query, w_key, w_value):
    return jnp.stack(
        [
            jnp.dot(normed, w_query, preferred_element_type=jnp.float32),
            jnp.dot(normed, w_key, preferred_element_type=jnp.float32),
            jnp.dot(normed, w_value, preferred_element_type=jnp.float32),
        ],
        axis=0,
    )


def project_two(normed, w_gate, w_up):
    return jnp.stack(
        [
            jnp.dot(normed, w_gate, preferred_element_type=jnp.float32),
            jnp.dot(normed, w_up, preferred_element_type=jnp.float32),
        ],
        axis=0,
    )


def attend(projected, cosine_table, sine_table, causal):
    length = projected.shape[1]
    local_head_count = projected.shape[2] // HEAD_DIM
    query_rot = rotate(
        projected[0].reshape(length, local_head_count, HEAD_DIM), cosine_table, sine_table
    ).astype(jnp.bfloat16)
    key_rot = rotate(
        projected[1].reshape(length, local_head_count, HEAD_DIM), cosine_table, sine_table
    ).astype(jnp.bfloat16)
    value_proj = projected[2].astype(jnp.bfloat16).reshape(length, local_head_count, HEAD_DIM)
    scores = jnp.einsum(
        "qhd,khd->hqk", query_rot, key_rot, preferred_element_type=jnp.float32
    ) * HEAD_DIM ** (-0.5)
    scores = jnp.where(causal[None], scores, -jnp.inf)
    weights_soft = jax.nn.softmax(scores, axis=-1).astype(jnp.bfloat16)
    attended = jnp.einsum(
        "hqk,khd->qhd", weights_soft, value_proj, preferred_element_type=jnp.float32
    )
    return attended.astype(jnp.bfloat16).reshape(length, local_head_count * HEAD_DIM)


def activate(projected):
    return (jax.nn.silu(projected[0]) * projected[1]).astype(jnp.bfloat16)


def tensor_total(term_rows):
    return lax.psum(term_rows.astype(jnp.bfloat16), "tensor").astype(jnp.float32)


def layer_whole(hidden, layer_weights, cosine_table, sine_table, causal):
    gain_attn, w_query, w_key, w_value, w_out, gain_mlp, w_gate, w_up, w_down = layer_weights
    normed = rms_norm(hidden, gain_attn)
    attended = attend(
        project_three(normed, w_query, w_key, w_value), cosine_table, sine_table, causal
    )
    attn_sum = tensor_total(jnp.dot(attended, w_out, preferred_element_type=jnp.float32))
    middle = (hidden.astype(jnp.float32) + attn_sum).astype(jnp.bfloat16)
    inner_act = activate(project_two(rms_norm(middle, gain_mlp), w_gate, w_up))
    mlp_sum = tensor_total(jnp.dot(inner_act, w_down, preferred_element_type=jnp.float32))
    return (middle.astype(jnp.float32) + mlp_sum).astype(jnp.bfloat16)


def body(
    ids_beam,
    beam_map,
    lengths,
    embed_table,
    gain_attn,
    w_query,
    w_key,
    w_value,
    w_out,
    gain_mlp,
    w_gate,
    w_up,
    w_down,
    final_gain,
    score_weight,
):
    section_index = lax.axis_index("section")
    batch_index = lax.axis_index("batch")
    tensor_index = lax.axis_index("tensor")
    per_device = ids_beam.shape[0]
    length = ids_beam.shape[1]
    all_cands = beam_map.shape[0]
    owned_cands = batch_index * per_device + jnp.arange(per_device, dtype=jnp.int32)
    matches = jnp.arange(all_cands, dtype=jnp.int32)[None, :] == owned_cands[:, None]
    beams_owned = jnp.sum(jnp.where(matches, beam_map[None, :], 0), axis=1)
    lengths_owned = jnp.sum(jnp.where(matches, lengths[None, :], 0), axis=1)
    looked = jnp.take(embed_table, ids_beam, axis=0)
    every_beam = lax.all_gather(looked, "batch", axis=0, tiled=True)
    picked = jnp.take(every_beam, beams_owned, axis=0)
    embedded = lax.all_gather(picked, ("section", "tensor"), axis=2, tiled=True)
    stacked = (gain_attn, w_query, w_key, w_value, w_out, gain_mlp, w_gate, w_up, w_down)
    layer_weights = tuple((tensor_arg[0] for tensor_arg in stacked))
    cosine_table, sine_table = rope_tables(length, HEAD_DIM)
    token_positions = jnp.arange(length)
    causal = token_positions[:, None] >= token_positions[None, :]
    share_rows = length // lax.axis_size("tensor")
    incoming = jnp.zeros((length, embedded.shape[2]), jnp.bfloat16)
    results = []
    for step_index in range(per_device + 1):
        source = embedded[min(step_index, per_device - 1)]
        current = jnp.where(section_index == 0, source, incoming)
        produced_rows = layer_whole(current, layer_weights, cosine_table, sine_table, causal)
        if step_index < per_device:
            incoming = shifted(produced_rows, "section", 1)
        if step_index >= 1:
            results.append(produced_rows)
    finals = jnp.stack(results, axis=0)
    own_rows = lax.dynamic_slice_in_dim(finals, tensor_index * share_rows, share_rows, 1)
    pooled = jnp.take_along_axis(finals, (lengths_owned - 1)[:, None, None], axis=1)[:, 0, :]
    half_width = own_rows.shape[2] // lax.axis_size("section")
    keep_half = lax.dynamic_slice_in_dim(own_rows, section_index * half_width, half_width, 2)
    received_half, received_pooled = shifted((own_rows[:, :, :half_width], pooled), "section", -1)
    first_section = section_index == 0
    shown_rows = jnp.where(first_section, received_half, keep_half)
    shown_pooled = jnp.where(first_section, received_pooled, pooled)
    scores = final_score(shown_pooled, final_gain, score_weight)
    return (shown_rows, scores)


def solution(mesh):
    placed = (
        P("batch", None),
        P(),
        P(),
        P(None, ("section", "tensor")),
        P("section", None),
        P("section", None, "tensor"),
        P("section", None, "tensor"),
        P("section", None, "tensor"),
        P("section", "tensor", None),
        P("section", None),
        P("section", None, "tensor"),
        P("section", None, "tensor"),
        P("section", "tensor", None),
        P(),
        P(),
    )
    return jax.shard_map(
        body,
        mesh=mesh,
        in_specs=placed,
        out_specs=(P("batch", "tensor", "section"), P("batch")),
        check_vma=False,
    )
```

profile of v0, /device:TPU:0, one launch (start us, length us, event | category | flops | bytes accessed | tf_op | source)
XLA Modules:
  0.0 956.4 jit_solution(13317318694306459853)
XLA Ops:
  8.6 9.8 %gather_fusion = bf16[512,512]{1,0:T(8,128)(2,1)S(1)} fusion(bf16[16000,512]{1,0:T(8,128)(2,1)} %param.18, s32[1024]{0:T(1024)S(1)} %pad_clamp_fusion.1), kind=kCustom, calls=%fused_computation | custom fusion | bytes 1050624 | tf_op jit(solution)/shard_map/jit(_take)/gather | solution.py:144
  20.2 24.6 %all-gather.3.cloned.1.call-done = bf16[8,256,512]{2,1,0:T(8,128)(2,1)} async-done(((bf16[2,256,512]{2,1,0:T(8,128)(2,1)}), bf16[8,256,512]{2,1,0:T(8,128)(2,1)}) %all-gather.3.cloned.1.call-update) | async-done | bytes 2097168 | tf_op jit(solution)/shard_map/all_gather | solution.py:145
  48.5 11.5 %copy.94 = bf16[1024,4096]{1,0:T(8,128)(2,1)} copy(bf16[1024,4096]{0,1:T(8,128)(2,1)} %bitcast.155) | data formatting | bytes 16777216 | tf_op jit(solution)/shard_map/dot_general | solution.py:57
  59.9 11.3 %copy.95 = bf16[1024,4096]{1,0:T(8,128)(2,1)} copy(bf16[1024,4096]{0,1:T(8,128)(2,1)} %bitcast.156) | data formatting | bytes 16777216 | tf_op jit(solution)/shard_map/dot_general | solution.py:58
  71.5 51.5 %all-gather.5.cloned.1.call-done = bf16[2,256,4096]{2,1,0:T(8,128)(2,1)} async-done(((bf16[2,256,512]{2,1,0:T(8,128)(2,1)}), bf16[2,256,4096]{2,1,0:T(8,128)(2,1)}) %all-gather.5.cloned.1.call-update) | async-done | bytes 4194320 | tf_op jit(solution)/shard_map/all_gather | solution.py:147
  125.3 6.4 fusion.100
  132.0 6.6 fusion.94
  138.6 5.8 fusion.92
  148.9 7.2 fusion.35
  156.8 84.1 %all-reduce.7.cloned.1.call-done = bf16[256,4096]{1,0:T(8,128)(2,1)} async-done(((bf16[256,4096]{1,0:T(8,128)(2,1)}), bf16[256,4096]{1,0:T(8,128)(2,1)}) %all-reduce.7.cloned.1.call-update) | async-done | bytes 2097168 | tf_op jit(solution)/shard_map/psum | solution.py:101
  244.4 8.3 fusion.19
  253.8 4.7 fusion.80
  258.5 11.6 %fusion.44 = bf16[256,4096]{1,0:T(8,128)(2,1)} fusion(bf16[256,2048]{1,0:T(8,128)(2,1)S(1)} %fusion.80, bf16[1,2048,4096]{2,1,0:T(8,128)(2,1)} %param.27), kind=kOutput, calls=%fused_computation.63 | convolution fusion | flops 4296015872 | bytes 19922944 | tf_op jit(solution)/shard_map/dot_general | solution.py:113
  270.1 85.6 %all-reduce.9.cloned.1.call-done = bf16[256,4096]{1,0:T(8,128)(2,1)} async-done(((bf16[256,4096]{1,0:T(8,128)(2,1)}), bf16[256,4096]{1,0:T(8,128)(2,1)}) %all-reduce.9.cloned.1.call-update) | async-done | bytes 2097168 | tf_op jit(solution)/shard_map/psum | solution.py:101
  362.0 44.5 %collective-permute-done = bf16[256,4096]{1,0:T(8,128)(2,1)S(1)} collective-permute-done((bf16[256,4096]{1,0:T(8,128)(2,1)S(1)}, bf16[256,4096]{1,0:T(8,128)(2,1)S(1)}, u32[]{:S(2)}, u32[]{:S(2)}) %collective-permute-start) | collective-permute-done | bytes 2097184 | tf_op jit(solution)/shard_map/ppermute | solution.py:14
  407.5 6.1 fusion.90
  424.7 4.0 fusion.230
  430.6 7.2 fusion.38
  438.2 86.4 %all-reduce.11.cloned.1.call-done = bf16[256,4096]{1,0:T(8,128)(2,1)} async-done(((bf16[256,4096]{1,0:T(8,128)(2,1)}), bf16[256,4096]{1,0:T(8,128)(2,1)}) %all-reduce.11.cloned.1.call-update) | async-done | bytes 2097168 | tf_op jit(solution)/shard_map/psum | solution.py:101
  527.4 9.0 fusion.17
  537.4 4.7 fusion.11
  542.1 11.8 %fusion.47 = bf16[256,4096]{1,0:T(8,128)(2,1)} fusion(bf16[1,2048,4096]{2,1,0:T(8,128)(2,1)} %param.27, f32[256,2048]{1,0:T(8,128)S(1)} %fusion.11, f32[256,2048]{1,0:T(8,128)S(1)} %fusion.17), kind=kOutput, calls=%fused_computation.64 | convolution fusion | flops 4299161600 | bytes 23068672 | tf_op jit(solution)/shard_map/dot_general | solution.py:113
  554.0 85.6 %all-reduce.13.cloned.1.call-done = bf16[256,4096]{1,0:T(8,128)(2,1)} async-done(((bf16[256,4096]{1,0:T(8,128)(2,1)}), bf16[256,4096]{1,0:T(8,128)(2,1)}) %all-reduce.13.cloned.1.call-update) | async-done | bytes 2097168 | tf_op jit(solution)/shard_map/psum | solution.py:101
  646.4 44.6 %collective-permute-done.1 = bf16[256,4096]{1,0:T(8,128)(2,1)S(1)} collective-permute-done((bf16[256,4096]{1,0:T(8,128)(2,1)S(1)}, bf16[256,4096]{1,0:T(8,128)(2,1)S(1)}, u32[]{:S(2)}, u32[]{:S(2)}) %collective-permute-start.1) | collective-permute-done | bytes 2097184 | tf_op jit(solution)/shard_map/ppermute | solution.py:14
  692.0 6.9 fusion.86
  715.2 7.1 fusion.41
  722.5 86.6 %all-reduce.15.cloned.1.call-done = bf16[256,4096]{1,0:T(8,128)(2,1)} async-done(((bf16[256,4096]{1,0:T(8,128)(2,1)}), bf16[256,4096]{1,0:T(8,128)(2,1)}) %all-reduce.15.cloned.1.call-update) | async-done | bytes 2097168 | tf_op jit(solution)/shard_map/psum | solution.py:101
  812.5 9.0 fusion.15
  822.6 4.7 fusion.9
  827.3 11.7 %fusion.50 = bf16[256,4096]{1,0:T(8,128)(2,1)} fusion(bf16[1,2048,4096]{2,1,0:T(8,128)(2,1)} %param.27, f32[256,2048]{1,0:T(8,128)S(1)} %fusion.9, f32[256,2048]{1,0:T(8,128)S(1)} %fusion.15), kind=kOutput, calls=%fused_computation.65 | convolution fusion | flops 4299161600 | bytes 23068672 | tf_op jit(solution)/shard_map/dot_general | solution.py:113
  839.8 84.9 %all-reduce.17.cloned.1.call-done = bf16[256,4096]{1,0:T(8,128)(2,1)} async-done(((bf16[256,4096]{1,0:T(8,128)(2,1)}), bf16[256,4096]{1,0:T(8,128)(2,1)}) %all-reduce.17.cloned.1.call-update) | async-done | bytes 2097168 | tf_op jit(solution)/shard_map/psum | solution.py:101
  934.6 11.6 %collective-permute-done.3 = bf16[2,4096]{1,0:T(2,128)(2,1)S(1)} collective-permute-done((bf16[2,4096]{1,0:T(2,128)(2,1)S(1)}, bf16[2,4096]{1,0:T(2,128)(2,1)S(1)}, u32[]{:S(2)}, u32[]{:S(2)}) %collective-permute-start.3) | collective-permute-done | bytes 16416 | tf_op jit(solution)/shard_map/ppermute | solution.py:14
  (170 shorter events, 86.0 us)
Async XLA Ops:
  7.2 37.6 %all-gather.3.cloned.1.call-start = ((), (), s32[]{:S(2)}) async-start(), calls=%async_computation | async-start | bytes 2621440 | tf_op jit(solution)/shard_map/all_gather | solution.py:145
  8.6 10.8 %copy-start.17 = (s32[8]{0:T(128)S(1)}, s32[8]{0:T(128)}, u32[]{:S(2)}) copy-start(s32[8]{0:T(128)} %param.17) | copy-start | bytes 100
  8.6 10.8 %copy-start.18 = (s32[8]{0:T(128)S(1)}, s32[8]{0:T(128)}, u32[]{:S(2)}) copy-start(s32[8]{0:T(128)} %param.16) | copy-start | bytes 100
  18.4 30.0 %copy-start.10 = (bf16[1,4096]{1,0:T(2,128)(2,1)S(1)}, bf16[1,4096]{1,0:T(2,128)(2,1)}, u32[]{:S(2)}) copy-start(bf16[1,4096]{1,0:T(2,128)(2,1)} %param.19) | copy-start | bytes 24580
  19.4 103.7 %all-gather.5.cloned.1.call-start = ((), (), s32[]{:S(2)}) async-start(), calls=%async_computation.1 | async-start | bytes 4718592 | tf_op jit(solution)/shard_map/all_gather | solution.py:147
  47.9 193.0 %all-reduce.7.cloned.1.call-start = ((), (), s32[]{:S(2)}) async-start(), calls=%async_computation.2 | async-start | bytes 4194304 | tf_op jit(solution)/shard_map/psum | solution.py:101
  71.2 73.5 %copy-start.9 = (pred[256,256]{0,1:T(8,128)(4,1)}, pred[256,256]{0,1:T(8,128)(4,1)S(1)}, u32[]{:S(2)}) copy-start(pred[256,256]{0,1:T(8,128)(4,1)S(1)} %iota_compare_fusion) | copy-start | bytes 196612
  156.0 199.7 %all-reduce.9.cloned.1.call-start = ((), (), s32[]{:S(2)}) async-start(), calls=%async_computation.3 | async-start | bytes 4194304 | tf_op jit(solution)/shard_map/psum | solution.py:101
  156.8 96.0 %copy-start.12 = (f32[1,4096]{1,0:T(1,128)}, f32[1,4096]{1,0:T(1,128)S(1)}, u32[]{:S(2)}) copy-start(f32[1,4096]{1,0:T(1,128)S(1)} %mul.617) | copy-start | bytes 49156
  240.9 11.9 %slice-start.4 = ((s8[16777216]{0:T(1024)(128)(4,1)}), s8[4194304]{0:T(1024)(128)(4,1)S(1)}, s32[]{:S(2)}) async-start(s8[16777216]{0:T(1024)(128)(4,1)} %bitcast.190), calls=%async_computation.12 | async-start | bytes 8388608
  244.4 9.4 slice-start.7
  270.1 254.5 %all-reduce.11.cloned.1.call-start = ((), (), s32[]{:S(2)}) async-start(), calls=%async_computation.4 | async-start | bytes 4194304 | tf_op jit(solution)/shard_map/psum | solution.py:101
  355.7 50.8 %copy-start.2 = (bf16[2,256,4096]{2,1,0:T(8,128)(2,1)S(1)}, bf16[2,256,4096]{2,1,0:T(8,128)(2,1)}, u32[]{:S(2)}) copy-start(bf16[2,256,4096]{2,1,0:T(8,128)(2,1)} %all-gather.5.cloned.1.call-done) | copy-start | bytes 12582916
  358.2 48.3 %collective-permute-start = (bf16[256,4096]{1,0:T(8,128)(2,1)S(1)}, bf16[256,4096]{1,0:T(8,128)(2,1)S(1)}, u32[]{:S(2)}, u32[]{:S(2)}) collective-permute-start(bf16[256,4096]{1,0:T(8,128)(2,1)S(1)} %fusion.60), channel_id=1, source_target_pairs={{0,16},{1,17},{2,18},{3,19},{4,20},{5,21},{6,22},{7,23},{8,24},{9,... | collective-permute-start | bytes 6291464 | tf_op jit(solution)/shard_map/ppermute | solution.py:14
  407.5 9.6 %slice-start.16 = ((s8[8388608]{0:T(1024)(128)(4,1)}), s8[4194304]{0:T(1024)(128)(4,1)S(1)}, s32[]{:S(2)}) async-start(s8[8388608]{0:T(1024)(128)(4,1)} %bitcast.196), calls=%async_computation.24 | async-start | bytes 8388608
  437.8 89.6 %copy-start.13 = (f32[1,4096]{1,0:T(1,128)S(1)}, f32[1,4096]{1,0:T(1,128)}, u32[]{:S(2)}) copy-start(f32[1,4096]{1,0:T(1,128)} %copy-done.12) | copy-start | bytes 49156
  437.8 201.8 %all-reduce.13.cloned.1.call-start = ((), (), s32[]{:S(2)}) async-start(), calls=%async_computation.5 | async-start | bytes 4194304 | tf_op jit(solution)/shard_map/psum | solution.py:101
  524.6 11.8 %slice-start.8 = ((s8[16777216]{0:T(1024)(128)(4,1)}), s8[4194304]{0:T(1024)(128)(4,1)S(1)}, s32[]{:S(2)}) async-start(s8[16777216]{0:T(1024)(128)(4,1)} %bitcast.192), calls=%async_computation.16 | async-start | bytes 8388608
  527.4 10.1 %slice-start.11 = ((s8[16777216]{0:T(1024)(128)(4,1)}), s8[4194304]{0:T(1024)(128)(4,1)S(1)}, s32[]{:S(2)}) async-start(s8[16777216]{0:T(1024)(128)(4,1)} %bitcast.192), calls=%async_computation.19 | async-start | bytes 8388608
  553.9 255.2 %all-reduce.15.cloned.1.call-start = ((), (), s32[]{:S(2)}) async-start(), calls=%async_computation.6 | async-start | bytes 4194304 | tf_op jit(solution)/shard_map/psum | solution.py:101
  639.5 51.4 %copy-start.3 = (bf16[2,256,4096]{2,1,0:T(8,128)(2,1)S(1)}, bf16[2,256,4096]{2,1,0:T(8,128)(2,1)}, u32[]{:S(2)}) copy-start(bf16[2,256,4096]{2,1,0:T(8,128)(2,1)} %all-gather.5.cloned.1.call-done) | copy-start | bytes 12582916
  642.7 48.3 %collective-permute-start.1 = (bf16[256,4096]{1,0:T(8,128)(2,1)S(1)}, bf16[256,4096]{1,0:T(8,128)(2,1)S(1)}, u32[]{:S(2)}, u32[]{:S(2)}) collective-permute-start(bf16[256,4096]{1,0:T(8,128)(2,1)S(1)} %fusion.68), channel_id=1, source_target_pairs={{0,16},{1,17},{2,18},{3,19},{4,20},{5,21},{6,22},{7,23},{8,24},{9,... | collective-permute-start | bytes 6291464 | tf_op jit(solution)/shard_map/ppermute | solution.py:14
  691.9 10.4 %copy-start.6 = (bf16[256,4096]{1,0:T(8,128)(2,1)}, bf16[256,4096]{1,0:T(8,128)(2,1)S(1)}, u32[]{:S(2)}) copy-start(bf16[256,4096]{1,0:T(8,128)(2,1)S(1)} %get-tuple-element.7) | copy-start | bytes 6291460
  691.9 10.4 %slice-start.18 = ((s8[8388608]{0:T(1024)(128)(4,1)}), s8[4194304]{0:T(1024)(128)(4,1)S(1)}, s32[]{:S(2)}) async-start(s8[8388608]{0:T(1024)(128)(4,1)} %bitcast.198), calls=%async_computation.26 | async-start | bytes 8388608
  722.3 90.2 %copy-start.14 = (f32[1,4096]{1,0:T(1,128)S(1)}, f32[1,4096]{1,0:T(1,128)}, u32[]{:S(2)}) copy-start(f32[1,4096]{1,0:T(1,128)} %copy-done.12) | copy-start | bytes 49156
  722.3 202.4 %all-reduce.17.cloned.1.call-start = ((), (), s32[]{:S(2)}) async-start(), calls=%async_computation.7 | async-start | bytes 4194304 | tf_op jit(solution)/shard_map/psum | solution.py:101
  809.1 12.4 %slice-start.12 = ((s8[16777216]{0:T(1024)(128)(4,1)}), s8[4194304]{0:T(1024)(128)(4,1)S(1)}, s32[]{:S(2)}) async-start(s8[16777216]{0:T(1024)(128)(4,1)} %bitcast.194), calls=%async_computation.20 | async-start | bytes 8388608
  812.4 9.1 copy-start.4
  812.5 9.1 slice-start.13
  812.5 10.1 %slice-start.15 = ((s8[16777216]{0:T(1024)(128)(4,1)}), s8[4194304]{0:T(1024)(128)(4,1)S(1)}, s32[]{:S(2)}) async-start(s8[16777216]{0:T(1024)(128)(4,1)} %bitcast.194), calls=%async_computation.23 | async-start | bytes 8388608
  930.3 16.9 %collective-permute-start.2 = (bf16[2,64,2048]{2,1,0:T(8,128)(2,1)S(1)}, bf16[2,64,2048]{2,1,0:T(8,128)(2,1)S(1)}, u32[]{:S(2)}, u32[]{:S(2)}) collective-permute-start(bf16[2,64,2048]{2,1,0:T(8,128)(2,1)S(1)} %fusion.128), channel_id=1, source_target_pairs={{16,0},{17,1},{18,2},{19,3},{20,4},{21,5},{22,6},{23,7},{24,8},{25... | collective-permute-start | bytes 1572872 | tf_op jit(solution)/shard_map/ppermute | solution.py:14
  933.3 13.0 %collective-permute-start.3 = (bf16[2,4096]{1,0:T(2,128)(2,1)S(1)}, bf16[2,4096]{1,0:T(2,128)(2,1)S(1)}, u32[]{:S(2)}, u32[]{:S(2)}) collective-permute-start(bf16[2,4096]{1,0:T(2,128)(2,1)S(1)} %broadcast_select_fusion.4), channel_id=1, source_target_pairs={{16,0},{17,1},{18,2},{19,3},{20,4},{21,5},{22,6},{23,7},{24,8},{25... | collective-permute-start | bytes 49160 | tf_op jit(solution)/shard_map/ppermute | solution.py:14
  (20 other events, 114.5 us)
Sparse Core Ops, SparseCore 0:
  19.5 25.2 all-gather.2
  48.0 75.0 all-gather.4
  156.2 84.6 all-reduce.6
  270.2 85.4 all-reduce.8
  437.9 86.6 all-reduce.10
  554.0 85.4 all-reduce.12
  722.4 86.6 all-reduce.14
  839.2 85.4 all-reduce.16
where the time goes:
time: 961 us; the launch traced here: 956 us
  waiting for transfers between devices  690 us (72%)
  matrix products  157 us (16%)
  local copies, waits for them, and re-layouts  44.9 us (5%)
  other arithmetic  37.3 us (4%)
  between operations  15.2 us (2%)
  starting transfers between devices  11.6 us (1%)
    psum x6, waiting for transfers between devices, tensor_total(): lax.psum(term_rows.astype(jnp.bfloat16), 'tensor').astype(jnp.float32)  513 us
    ppermute x4, waiting for transfers between devices, shifted(): lax.ppermute(value, axis, [(source, source + steps) for source in range(l...  101 us
    all_gather x1, waiting for transfers between devices, body(): embedded = lax.all_gather(picked, ('section', 'tensor'), axis=2, tiled=True)  51.5 us
    dot_general x3, matrix products, layer_whole(): jnp.dot(inner_act, w_down, preferred_element_type=jnp.float32)  35.1 us
    dot_general x3, matrix products, project_two(): jnp.dot(normed, w_gate, preferred_element_type=jnp.float32)  26.3 us
    all_gather x1, waiting for transfers between devices, body(): every_beam = lax.all_gather(looked, 'batch', axis=0, tiled=True)  24.6 us
    dot_general x3, matrix products, layer_whole(): jnp.dot(attended, w_out, preferred_element_type=jnp.float32)  21.4 us
    dot_general x3, matrix products, project_three(): jnp.dot(normed, w_query, preferred_element_type=jnp.float32)  19.6 us
  transfers between devices with their start and end apart: 12, of which 11 were waited for; matrix products, arithmetic and copies ran while one was open for 3% of the time, Pallas kernels for 0%

commit v1 on v0

--- a/solution.py
+++ b/solution.py
@@ -98,7 +98,9 @@
 
 
 def tensor_total(term_rows):
-    return lax.psum(term_rows.astype(jnp.bfloat16), "tensor").astype(jnp.float32)
+    return jnp.sum(lax.all_gather(term_rows.astype(jnp.bfloat16), "tensor"), axis=0).astype(
+        jnp.float32
+    )
 
 
 def layer_whole(hidden, layer_weights, cosine_table, sine_table, causal):

time: 961 us -> 1380 us (1.44)
  waiting for transfers between devices: 690 us -> 1070 us
  other arithmetic: 37.3 us -> 77.1 us
    all_gather x0 -> x6, waiting for transfers between devices: none -> 889 us  [tensor_total(): lax.all_gather(term_rows.astype(jnp.bfloat16), 'tensor')]
    psum x6 -> x0, waiting for transfers between devices: 513 us -> none  [tensor_total(): lax.psum(term_rows.astype(jnp.bfloat16), 'tensor').astype(jnp.float32)]
    reduce_sum x0 -> x6, other arithmetic: none -> 39.7 us  [tensor_total(): jnp.sum(lax.all_gather(term_rows.astype(jnp.bfloat16), 'tensor'), axis=0)]
  transfers between devices with their start and end apart: 12 -> 12, of which waited for: 11 -> 11; matrix products, arithmetic and copies ran while one was open for 3% -> 2% of each run, Pallas kernels for 0% -> 0%
where the time goes in v1:
time: 1380 us; the launch traced here: 1370 us
  waiting for transfers between devices  1070 us (78%)
  matrix products  160 us (12%)
  other arithmetic  77.1 us (6%)
  local copies, waits for them, and re-layouts  42.9 us (3%)
  between operations  15.1 us (1%)
    all_gather x6, waiting for transfers between devices, tensor_total(): lax.all_gather(term_rows.astype(jnp.bfloat16), 'tensor')  889 us
    ppermute x4, waiting for transfers between devices, shifted(): lax.ppermute(value, axis, [(source, source + steps) for source in range(l...  101 us
    all_gather x1, waiting for transfers between devices, body(): embedded = lax.all_gather(picked, ('section', 'tensor'), axis=2, tiled=True)  51.9 us
    dot_general x3, matrix products, layer_whole(): jnp.dot(inner_act, w_down, preferred_element_type=jnp.float32)  41.6 us
    reduce_sum x6, other arithmetic, tensor_total(): jnp.sum(lax.all_gather(term_rows.astype(jnp.bfloat16), 'tensor'), axis=0)  39.7 us
  transfers between devices with their start and end apart: 12, of which 11 were waited for; matrix products, arithmetic and copies ran while one was open for 2% of the time, Pallas kernels for 0%

profile of v1, /device:TPU:0, one launch (start us, length us, event | category | flops | bytes accessed | tf_op | source)
XLA Modules:
  0.0 1373.2 jit_solution(10593054818227556770)
XLA Ops:
  8.6 9.8 gather_fusion
  20.2 24.6 %all-gather.15.cloned.1.call-done = bf16[8,256,512]{2,1,0:T(8,128)(2,1)} async-done(((bf16[2,256,512]{2,1,0:T(8,128)(2,1)}), bf16[8,256,512]{2,1,0:T(8,128)(2,1)}) %all-gather.15.cloned.1.call-update) | async-done | bytes 2097168 | tf_op jit(solution)/shard_map/all_gather | solution.py:147
  48.2 11.4 copy.94
  59.5 11.3 copy.95
  71.2 51.9 %all-gather.17.cloned.1.call-done = bf16[2,256,4096]{2,1,0:T(8,128)(2,1)} async-done(((bf16[2,256,512]{2,1,0:T(8,128)(2,1)}), bf16[2,256,4096]{2,1,0:T(8,128)(2,1)}) %all-gather.17.cloned.1.call-update) | async-done | bytes 4194320 | tf_op jit(solution)/shard_map/all_gather | solution.py:149
  125.3 6.4 fusion.100
  131.9 6.6 fusion.94
  148.8 7.1 fusion.35
  156.2 147.7 %all-gather.19.cloned.1.call-done = bf16[1024,4096]{1,0:T(8,128)(2,1)} async-done(((bf16[256,4096]{1,0:T(8,128)(2,1)}), bf16[1024,4096]{1,0:T(8,128)(2,1)}) %all-gather.19.cloned.1.call-update) | async-done | bytes 8388624 | tf_op jit(solution)/shard_map/all_gather | solution.py:101
  311.9 9.5 fusion.19
  321.4 18.0 %fusion.44 = bf16[256,4096]{1,0:T(8,128)(2,1)} fusion(bf16[1,2048,4096]{2,1,0:T(8,128)(2,1)} %param.27, bf16[1,4096,2048]{2,1,0:T(8,128)(2,1)} %param.26, f32[256,2048]{1,0:T(8,128)} %fusion.19, bf16[256,4096]{1,0:T(8,128)(2,1)S(1)} %reduce_sum.195, f32[4096]{0:T(1024)S(1)} %bitcast.218, f32[256]{0:T(256)S(1)} %add_rsqrt_fusion.4, ...), kind=kOutput, calls=%fused_computation.64 | convolution fusion | flops 8603566080 | bytes 41960448 | tf_op jit(solution)/shard_map/dot_general | solution.py:115
  339.5 148.0 %all-gather.21.cloned.1.call-done = bf16[1024,4096]{1,0:T(8,128)(2,1)} async-done(((bf16[256,4096]{1,0:T(8,128)(2,1)}), bf16[1024,4096]{1,0:T(8,128)(2,1)}) %all-gather.21.cloned.1.call-update) | async-done | bytes 8388624 | tf_op jit(solution)/shard_map/all_gather | solution.py:101
  487.5 6.9 reduce_sum.197
  501.8 44.5 %collective-permute-done = bf16[256,4096]{1,0:T(8,128)(2,1)S(1)} collective-permute-done((bf16[256,4096]{1,0:T(8,128)(2,1)S(1)}, bf16[256,4096]{1,0:T(8,128)(2,1)S(1)}, u32[]{:S(2)}, u32[]{:S(2)}) %collective-permute-start) | collective-permute-done | bytes 2097184 | tf_op jit(solution)/shard_map/ppermute | solution.py:14
  547.3 6.1 fusion.90
  570.4 7.1 fusion.38
  577.7 148.7 %all-gather.23.cloned.1.call-done = bf16[1024,4096]{1,0:T(8,128)(2,1)} async-done(((bf16[256,4096]{1,0:T(8,128)(2,1)}), bf16[1024,4096]{1,0:T(8,128)(2,1)}) %all-gather.23.cloned.1.call-update) | async-done | bytes 8388624 | tf_op jit(solution)/shard_map/all_gather | solution.py:101
  726.4 6.9 reduce_sum.200
  736.1 9.0 fusion.17
  750.8 11.8 fusion.47
  762.7 148.0 %all-gather.25.cloned.1.call-done = bf16[1024,4096]{1,0:T(8,128)(2,1)} async-done(((bf16[256,4096]{1,0:T(8,128)(2,1)}), bf16[1024,4096]{1,0:T(8,128)(2,1)}) %all-gather.25.cloned.1.call-update) | async-done | bytes 8388624 | tf_op jit(solution)/shard_map/all_gather | solution.py:101
  910.7 6.9 reduce_sum.202
  924.6 44.6 %collective-permute-done.1 = bf16[256,4096]{1,0:T(8,128)(2,1)S(1)} collective-permute-done((bf16[256,4096]{1,0:T(8,128)(2,1)S(1)}, bf16[256,4096]{1,0:T(8,128)(2,1)S(1)}, u32[]{:S(2)}, u32[]{:S(2)}) %collective-permute-start.1) | collective-permute-done | bytes 2097184 | tf_op jit(solution)/shard_map/ppermute | solution.py:14
  970.2 6.9 fusion.86
  993.4 7.2 fusion.41
  1000.8 148.7 %all-gather.27.cloned.1.call-done = bf16[1024,4096]{1,0:T(8,128)(2,1)} async-done(((bf16[256,4096]{1,0:T(8,128)(2,1)}), bf16[1024,4096]{1,0:T(8,128)(2,1)}) %all-gather.27.cloned.1.call-update) | async-done | bytes 8388624 | tf_op jit(solution)/shard_map/all_gather | solution.py:101
  1149.5 7.0 reduce_sum.205
  1159.9 9.0 fusion.15
  1174.7 11.7 fusion.50
  1186.6 147.9 %all-gather.29.cloned.1.call-done = bf16[1024,4096]{1,0:T(8,128)(2,1)} async-done(((bf16[256,4096]{1,0:T(8,128)(2,1)}), bf16[1024,4096]{1,0:T(8,128)(2,1)}) %all-gather.29.cloned.1.call-update) | async-done | bytes 8388624 | tf_op jit(solution)/shard_map/all_gather | solution.py:101
  1334.5 6.9 reduce_sum.207
  1351.3 11.8 collective-permute-done.3
  (168 shorter events, 108.5 us)
Async XLA Ops:
  7.2 12.3 copy-start.19
  7.2 12.3 copy-start.18
  7.2 37.6 %all-gather.15.cloned.1.call-start = ((), (), s32[]{:S(2)}) async-start(), calls=%async_computation | async-start | bytes 2621440 | tf_op jit(solution)/shard_map/all_gather | solution.py:147
  8.6 39.5 %copy-start.11 = (bf16[1,4096]{1,0:T(2,128)(2,1)S(1)}, bf16[1,4096]{1,0:T(2,128)(2,1)}, u32[]{:S(2)}) copy-start(bf16[1,4096]{1,0:T(2,128)(2,1)} %param.19) | copy-start | bytes 24580
  19.3 103.7 %all-gather.17.cloned.1.call-start = ((), (), s32[]{:S(2)}) async-start(), calls=%async_computation.1 | async-start | bytes 4718592 | tf_op jit(solution)/shard_map/all_gather | solution.py:149
  47.9 256.0 %all-gather.19.cloned.1.call-start = ((), (), s32[]{:S(2)}) async-start(), calls=%async_computation.2 | async-start | bytes 10485760 | tf_op jit(solution)/shard_map/all_gather | solution.py:101
  70.8 73.9 %copy-start.10 = (pred[256,256]{0,1:T(8,128)(4,1)}, pred[256,256]{0,1:T(8,128)(4,1)S(1)}, u32[]{:S(2)}) copy-start(pred[256,256]{0,1:T(8,128)(4,1)S(1)} %iota_compare_fusion) | copy-start | bytes 196612
  155.9 331.6 %all-gather.21.cloned.1.call-start = ((), (), s32[]{:S(2)}) async-start(), calls=%async_computation.3 | async-start | bytes 10485760 | tf_op jit(solution)/shard_map/all_gather | solution.py:101
  156.2 165.2 %copy-start.13 = (f32[1,4096]{1,0:T(1,128)}, f32[1,4096]{1,0:T(1,128)S(1)}, u32[]{:S(2)}) copy-start(f32[1,4096]{1,0:T(1,128)S(1)} %mul.623) | copy-start | bytes 49156
  339.5 386.9 %all-gather.23.cloned.1.call-start = ((), (), s32[]{:S(2)}) async-start(), calls=%async_computation.4 | async-start | bytes 10485760 | tf_op jit(solution)/shard_map/all_gather | solution.py:101
  494.4 51.9 %copy-start.3 = (bf16[2,256,4096]{2,1,0:T(8,128)(2,1)S(1)}, bf16[2,256,4096]{2,1,0:T(8,128)(2,1)}, u32[]{:S(2)}) copy-start(bf16[2,256,4096]{2,1,0:T(8,128)(2,1)} %all-gather.17.cloned.1.call-done) | copy-start | bytes 12582916
  497.8 48.5 %collective-permute-start = (bf16[256,4096]{1,0:T(8,128)(2,1)S(1)}, bf16[256,4096]{1,0:T(8,128)(2,1)S(1)}, u32[]{:S(2)}, u32[]{:S(2)}) collective-permute-start(bf16[256,4096]{1,0:T(8,128)(2,1)S(1)} %fusion.54), channel_id=1, source_target_pairs={{0,16},{1,17},{2,18},{3,19},{4,20},{5,21},{6,22},{7,23},{8,24},{9,... | collective-permute-start | bytes 6291464 | tf_op jit(solution)/shard_map/ppermute | solution.py:14
  547.3 9.6 slice-start.12
  577.5 333.2 %all-gather.25.cloned.1.call-start = ((), (), s32[]{:S(2)}) async-start(), calls=%async_computation.5 | async-start | bytes 10485760 | tf_op jit(solution)/shard_map/all_gather | solution.py:101
  733.3 11.8 slice-start.4
  736.0 9.1 copy-start.6
  736.1 9.1 slice-start.5
  736.1 10.1 slice-start.7
  762.7 386.9 %all-gather.27.cloned.1.call-start = ((), (), s32[]{:S(2)}) async-start(), calls=%async_computation.6 | async-start | bytes 10485760 | tf_op jit(solution)/shard_map/all_gather | solution.py:101
  917.6 51.6 %copy-start.4 = (bf16[2,256,4096]{2,1,0:T(8,128)(2,1)S(1)}, bf16[2,256,4096]{2,1,0:T(8,128)(2,1)}, u32[]{:S(2)}) copy-start(bf16[2,256,4096]{2,1,0:T(8,128)(2,1)} %all-gather.17.cloned.1.call-done) | copy-start | bytes 12582916
  920.7 48.5 %collective-permute-start.1 = (bf16[256,4096]{1,0:T(8,128)(2,1)S(1)}, bf16[256,4096]{1,0:T(8,128)(2,1)S(1)}, u32[]{:S(2)}, u32[]{:S(2)}) collective-permute-start(bf16[256,4096]{1,0:T(8,128)(2,1)S(1)} %fusion.64), channel_id=1, source_target_pairs={{0,16},{1,17},{2,18},{3,19},{4,20},{5,21},{6,22},{7,23},{8,24},{9,... | collective-permute-start | bytes 6291464 | tf_op jit(solution)/shard_map/ppermute | solution.py:14
  970.2 10.4 copy-start.7
  970.2 10.4 slice-start.14
  1000.6 333.9 %all-gather.29.cloned.1.call-start = ((), (), s32[]{:S(2)}) async-start(), calls=%async_computation.7 | async-start | bytes 10485760 | tf_op jit(solution)/shard_map/all_gather | solution.py:101
  1156.5 12.4 slice-start.8
  1159.8 9.1 copy-start.5
  1159.9 9.1 slice-start.9
  1159.9 9.1 slice-start.10
  1159.9 10.1 slice-start.11
  1174.7 11.8 copy-start.20
  1347.0 17.1 %collective-permute-start.2 = (bf16[2,64,2048]{2,1,0:T(8,128)(2,1)S(1)}, bf16[2,64,2048]{2,1,0:T(8,128)(2,1)S(1)}, u32[]{:S(2)}, u32[]{:S(2)}) collective-permute-start(bf16[2,64,2048]{2,1,0:T(8,128)(2,1)S(1)} %fusion.126), channel_id=1, source_target_pairs={{16,0},{17,1},{18,2},{19,3},{20,4},{21,5},{22,6},{23,7},{24,8},{25... | collective-permute-start | bytes 1572872 | tf_op jit(solution)/shard_map/ppermute | solution.py:14
  1350.0 13.2 collective-permute-start.3
  (17 other events, 85.4 us)
Sparse Core Ops, SparseCore 0:
  19.5 25.2 all-gather.14
  48.0 75.0 all-gather.16
  156.0 147.8 all-gather.18
  339.6 147.8 all-gather.20
  577.6 148.7 all-gather.22
  762.8 147.8 all-gather.24
  1000.7 148.7 all-gather.26
  1186.6 147.8 all-gather.28
